TPU v7x, 128 devices: a whole 4x4x4 slice. The times are simulated.
128 devices in a mesh: replica: 4 (over y_hi, core), fsdp: 32 (over y_lo, z, x).
Axes of the slice: x: 4, y: 4 (y_hi: 2, y_lo: 2; y = y_hi * 2 + y_lo), z: 4, core: 2. Of those that a mesh axis runs over, the one named last changes fastest.
Arguments:
- layer_input: bfloat16 [4, 16384, 4096], P('replica', 'fsdp'), may hold values from -36 to 36, as said below
- norm_gain: bfloat16 [4, 4096], P('replica', 'fsdp'), may hold values from 0.099609375 to 1.8984375
- kv_weight: bfloat16 [4, 4096, 1024], P('replica', 'fsdp'), may hold values from -0.09375 to 0.09375
- kv_cotangent: bfloat16 [4, 16384, 1024], P('replica', 'fsdp'), may hold values from -6 to 6
- pseudo_grad: float32 [4, 12288, 1024], P('replica', 'fsdp'), may hold values from -6 to 6
- outer_momentum: float32 [12288, 1024], P('fsdp'), may hold values from -6 to 6
- global_params: float32 [12288, 1024], P('fsdp'), may hold values from -6 to 6
- local_params: bfloat16 [4, 12288, 1024], P('replica', 'fsdp'), may hold values from -6 to 6
Outputs:
- kv_out: bfloat16 [4, 16384, 1024], P('replica', 'fsdp')
- input_grad: bfloat16 [4, 16384, 4096], P('replica', 'fsdp')
- kv_weight_grad: float32 [4, 4096, 1024], P('replica', 'fsdp')
- gain_grad: float32 [4, 4096], P('replica', 'fsdp')
- momentum_new: float32 [12288, 1024], P('fsdp')
- global_new: float32 [12288, 1024], P('fsdp')
- local_new: bfloat16 [4, 12288, 1024], P('replica', 'fsdp')
Inputs may be any that keep to these rules, and one draw needn't show every extreme that they name: `layer_input`: activations of the residual stream.
All inputs are finite; a program needn't handle non-finite values.
Results may differ from a plain program's by a relative error of at most 0.0049.
Values may be sent and summed in bfloat16 or wider, within the bound.
A program may use at most 128 MiB of HBM per device.

v0:
```python
import math
import jax
import jax.numpy as jnp
from jax import lax
from jax.sharding import PartitionSpec as P

HEAD = 128
SEQ_LEN = 4096
epsilon = 1e-05
rope_base = 500000.0
momentum_rate = 0.9
outer_rate = 0.7
mixing_rate = 0.5


def angles_for(positions, head):
    half = head // 2
    index_f = jnp.arange(half, dtype=jnp.float32)
    inverse = jnp.exp(index_f * (-2.0 * math.log(rope_base) / head))
    angle = positions.astype(jnp.float32)[:, None] * inverse[None, :]
    return (jnp.cos(angle), jnp.sin(angle))


def rotate_keys(keys, cosine, sine, head, sign):
    count = keys.shape[0]
    shaped = keys.reshape(count, -1, head)
    half = head // 2
    first = shaped[:, :, :half]
    second = shaped[:, :, half:]
    cos_b = cosine[:, None, :]
    sin_b = sine[:, None, :] * sign
    out = jnp.concatenate([first * cos_b - second * sin_b, second * cos_b + first * sin_b], axis=2)
    return out.reshape(count, -1)


def forward_piece(normed, weight_piece, gain_piece):
    gain_vals = gain_piece.astype(jnp.float32)
    hidden_piece = (normed * gain_vals[None, :]).astype(jnp.bfloat16)
    key_pre = jnp.dot(hidden_piece, weight_piece, preferred_element_type=jnp.float32)
    return (key_pre, hidden_piece, gain_vals)


def backward_piece(kv_grad, weight_piece):
    product = lax.dot_general(
        kv_grad, weight_piece, (((1,), (1,)), ((), ())), preferred_element_type=jnp.float32
    )
    return product


def local(
    layer_input,
    norm_gain,
    kv_weight,
    kv_cotangent,
    pseudo_grad,
    outer_momentum,
    global_params,
    local_params,
):
    tokens_in = layer_input[0]
    gain_shard = norm_gain[0]
    weight_shard = kv_weight[0]
    cotangent = kv_cotangent[0]
    rows, width = tokens_in.shape
    kvw = weight_shard.shape[1] // 2
    groups = lax.axis_size("fsdp")
    positions = (lax.axis_index("fsdp") * rows + jnp.arange(rows, dtype=jnp.int32)) % SEQ_LEN
    cosine, sine = angles_for(positions, HEAD)
    values = tokens_in.astype(jnp.float32)
    inv_rms = lax.rsqrt(jnp.mean(values * values, axis=-1, keepdims=True) + epsilon)
    normed = values * inv_rms
    key_back = rotate_keys(cotangent[:, :kvw].astype(jnp.float32), cosine, sine, HEAD, -1.0).astype(
        jnp.bfloat16
    )
    kv_grad = jnp.concatenate([key_back, cotangent[:, kvw:]], axis=1)
    key_pre, hidden, gain_full = forward_piece(
        normed,
        lax.all_gather(weight_shard, "fsdp", axis=0, tiled=True),
        lax.all_gather(gain_shard, "fsdp", axis=0, tiled=True),
    )
    hidden_grad = backward_piece(kv_grad, lax.all_gather(weight_shard, "fsdp", axis=0, tiled=True))
    kv_out = jnp.concatenate(
        [rotate_keys(key_pre[:, :kvw], cosine, sine, HEAD, 1.0), key_pre[:, kvw:]], axis=1
    ).astype(jnp.bfloat16)
    scale = 1.0 / math.sqrt(rows * groups)
    gain_product = hidden_grad * normed
    weight_term = (
        lax.dot_general(
            hidden, kv_grad, (((0,), (0,)), ((), ())), preferred_element_type=jnp.float32
        )
        * scale
    )
    gain_term = jnp.sum(gain_product, axis=0) * scale
    weight_grad, gain_grad = (
        lax.psum_scatter(weight_term, "fsdp", scatter_dimension=0, tiled=True),
        lax.psum_scatter(gain_term, "fsdp", scatter_dimension=0, tiled=True),
    )
    normed_grad = hidden_grad * gain_full
    input_grad = (
        inv_rms * (normed_grad - normed * jnp.mean(normed_grad * normed, axis=-1, keepdims=True))
    ).astype(jnp.bfloat16)
    pseudo = pseudo_grad[0]
    replicas = lax.axis_size("replica")
    total = lax.psum(pseudo, "replica")
    average = total / replicas
    momentum_new = momentum_rate * outer_momentum + average
    global_new = global_params - outer_rate * (average + momentum_rate * momentum_new)
    local_new = (
        mixing_rate * local_params[0].astype(jnp.float32) + (1.0 - mixing_rate) * global_new
    ).astype(jnp.bfloat16)
    return (
        kv_out[None],
        input_grad[None],
        weight_grad[None],
        gain_grad[None],
        momentum_new,
        global_new,
        local_new[None],
    )


def solution(mesh):
    in_specs = (
        P("replica", "fsdp", None),
        P("replica", "fsdp"),
        P("replica", "fsdp", None),
        P("replica", "fsdp", None),
        P("replica", "fsdp", None),
        P("fsdp", None),
        P("fsdp", None),
        P("replica", "fsdp", None),
    )
    out_specs = (
        P("replica", "fsdp", None),
        P("replica", "fsdp", None),
        P("replica", "fsdp", None),
        P("replica", "fsdp"),
        P("fsdp", None),
        P("fsdp", None),
        P("replica", "fsdp", None),
    )
    return jax.shard_map(local, mesh=mesh, in_specs=in_specs, out_specs=out_specs, check_vma=False)
```

profile of v0, /device:TPU:0, one launch (start us, length us, event | category | flops | bytes accessed | tf_op | source)
XLA Modules:
  0.0 415.8 jit_solution(27503207839580185)
XLA Ops:
  8.1 0.7 all-gather.4.cloned.1.call-update
  8.8 0.5 all-reduce.3.cloned.1.call-update
  9.4 82.9 %all-gather = bf16[1,4096]{1,0:T(2,128)(2,1)S(1)} all-gather(bf16[1,128]{1,0:T(2,128)(2,1)} %param.9), channel_id=2, replica_groups=mesh['replica'=4,'fsdp'=32] {'fsdp'}, dimensions={1}, use_global_device_ids=true | all-gather | bytes 8448 | tf_op jit(solution)/shard_map/all_gather | solution.py:79
  92.3 3.1 fusion.10
  95.5 0.9 slice_convert_fusion.1
  96.4 0.4 reshape.172
  96.8 1.8 broadcast_multiply_fusion.1
  98.6 80.9 %all-gather.4.cloned.1.call-done = bf16[1,4096,1024]{2,1,0:T(8,128)(2,1)} async-done(((bf16[1,128,1024]{2,1,0:T(8,128)(2,1)}), bf16[1,4096,1024]{2,1,0:T(8,128)(2,1)}) %all-gather.4.cloned.1.call-update) | async-done | bytes 8388624 | tf_op jit(solution)/shard_map/all_gather | solution.py:78
  179.5 8.2 %fusion.13 = f32[512,1024]{1,0:T(8,128)S(1)} fusion(bf16[1,4096,1024]{2,1,0:T(8,128)(2,1)} %all-gather.4.cloned.1.call-done, bf16[1,512,4096]{2,1,0:T(8,128)(2,1)} %param.8, f32[4096]{0:T(1024)S(1)} %bitcast.41, f32[512]{0:T(512)S(1)} %add_rsqrt_fusion), kind=kOutput, calls=%fused_computation.15 | convolution fusion | flops 4303355904 | bytes 14698496 | tf_op jit(solution)/shard_map/dot_general | solution.py:39
  187.7 1.3 copy-done.2
  189.1 0.4 reshape.167
  189.5 2.7 subtract_convert_fusion
  192.3 1.4 pad_maximum_fusion.4
  193.8 8.3 %broadcast_multiply_fusion = f32[4096,1024]{1,0:T(8,128)} fusion(bf16[1,512,4096]{2,1,0:T(8,128)(2,1)S(1)} %copy-done, f32[4096]{0:T(1024)S(1)} %bitcast.42, f32[512]{0:T(512)S(1)} %add_rsqrt_fusion, bf16[512,512]{1,0:T(8,128)(2,1)S(1)} %copy-done.5, bf16[512,512]{1,0:T(8,128)(2,1)S(1)} %bitcast.39), kind=kOutput, calls=%fused_computation.17 | convolution fusion | flops 4309647360 | bytes 22038528 | tf_op jit(solution)/shard_map/dot_general | solution.py:88
  202.1 0.6 copy-done.8
  202.8 0.6 dynamic-slice
  204.1 4.6 %fusion.20 = (bf16[1,384,1024]{2,1,0:T(8,128)(2,1)}, f32[384,1024]{1,0:T(8,128)}, f32[384,1024]{1,0:T(8,128)}) fusion(bf16[1,384,1024]{2,1,0:T(8,128)(2,1)S(1)} %copy-done.4, f32[384,1024]{1,0:T(8,128)S(1)} %copy-done.1, f32[384,1024]{1,0:T(8,128)} %all-reduce.3.cloned.1.call-done, f32[384,1024]{1,0:T(8,128)} %param.13), kind=kLoop, calls=%fused_computation.31 | loop fusion | flops 4325376 | bytes 9437184 | tf_op jit(solution)/shard_map/broadcast_in_dim | solution.py:118
  208.9 13.6 %fusion.9 = (f32[4096]{0:T(1024)S(1)}, f32[512]{0:T(512)S(1)}, f32[512,4096]{1,0:T(8,128)}) fusion(bf16[1,512,4096]{2,1,0:T(8,128)(2,1)} %param.8, f32[512]{0:T(512)S(1)} %add_rsqrt_fusion, f32[4096]{0:T(1024)S(1)} %bitcast.43, bf16[1,4096,1024]{2,1,0:T(8,128)(2,1)} %all-gather.4.cloned.1.call-done, bf16[512,512]{1,0:T(8,128)(2,1)S(1)} %copy-done.6, ...), kind=kOutput, calls=%fused_computation.11 | convolution fusion | flops 4311739904 | bytes 22056960 | tf_op jit(solution)/shard_map/dot_general | solution.py:44
  222.4 158.3 %all-reduce = f32[4096]{0:T(1024)S(1)} all-reduce(f32[4096]{0:T(1024)S(1)} %broadcast_multiply_fusion.2), channel_id=5, replica_groups=mesh['replica'=4,'fsdp'=32] {'fsdp'}, use_global_device_ids=true, to_apply=%region_4.5.clone | all-reduce | flops 4096 | bytes 32768
  380.8 0.6 dynamic-slice_bitcast_fusion
  381.3 1.3 fusion.21
  382.6 1.1 pad_maximum_fusion
  383.8 7.3 %fusion.15 = bf16[1,512,4096]{2,1,0:T(8,128)(2,1)} fusion(f32[512,4096]{1,0:T(8,128)} %get-tuple-element.23, bf16[1,512,4096]{2,1,0:T(8,128)(2,1)} %param.8, f32[512]{0:T(512)S(1)} %broadcast_multiply_fusion.3, f32[4096]{0:T(1024)S(1)} %bitcast.44, f32[512]{0:T(512)S(1)} %add_rsqrt_fusion), kind=kLoop, calls=%fused_computation.18 | loop fusion | flops 14680064 | bytes 16797696 | tf_op jit(solution)/shard_map/broadcast_in_dim | solution.py:113
  391.1 17.3 %reduce-scatter.2.cloned.1.call-done = f32[128,1024]{1,0:T(8,128)} async-done(((f32[4096,1024]{1,0:T(8,128)}), f32[128,1024]{1,0:T(8,128)}) %reduce-scatter.2.cloned.1.call-update) | async-done | bytes 524304 | tf_op jit(solution)/shard_map/reduce_scatter | solution.py:95
  (30 shorter events, 0.6 us)
Async XLA Ops:
  8.0 87.4 %copy-start.3 = (bf16[1,512,1024]{2,1,0:T(8,128)(2,1)S(1)}, bf16[1,512,1024]{2,1,0:T(8,128)(2,1)}, u32[]{:S(2)}) copy-start(bf16[1,512,1024]{2,1,0:T(8,128)(2,1)} %param.11) | copy-start | bytes 3145732
  8.0 171.5 %all-gather.4.cloned.1.call-start = ((), (), s32[]{:S(2)}) async-start(), calls=%async_computation.3 | async-start | bytes 8650752 | tf_op jit(solution)/shard_map/all_gather | solution.py:78
  8.7 195.3 %all-reduce.3.cloned.1.call-start = ((), (), s32[]{:S(2)}) async-start(), calls=%async_computation.2 | async-start | bytes 3145728 | tf_op jit(solution)/shard_map/psum | solution.py:104
  9.3 399.1 %reduce-scatter.2.cloned.1.call-start = ((), (), s32[]{:S(2)}) async-start(), calls=%async_computation.1 | async-start | bytes 17301504 | tf_op jit(solution)/shard_map/reduce_scatter | solution.py:95
  187.7 1.3 copy-start.2
  189.5 4.3 %copy-start = (bf16[1,512,4096]{2,1,0:T(8,128)(2,1)S(1)}, bf16[1,512,4096]{2,1,0:T(8,128)(2,1)}, u32[]{:S(2)}) copy-start(bf16[1,512,4096]{2,1,0:T(8,128)(2,1)} %param.8) | copy-start | bytes 12582916
  189.5 4.3 %copy-start.5 = (bf16[512,512]{1,0:T(8,128)(2,1)S(1)}, bf16[512,512]{1,0:T(8,128)(2,1)}, u32[]{:S(2)}) copy-start(bf16[512,512]{1,0:T(8,128)(2,1)} %get-tuple-element.17) | copy-start | bytes 1572868
  193.8 8.3 %copy-start.7 = (bf16[64,8,4,128]{3,1,2,0:T(8,128)(2,1)}, bf16[64,8,4,128]{3,1,2,0:T(8,128)(2,1)S(1)}, u32[]{:S(2)}) copy-start(bf16[64,8,4,128]{3,1,2,0:T(8,128)(2,1)S(1)} %copy.17) | copy-start | bytes 1572868
  202.1 0.7 copy-start.8
  202.1 1.9 copy-start.1
  202.1 1.9 copy-start.4
  204.0 4.9 %copy-start.6 = (bf16[512,512]{1,0:T(8,128)(2,1)S(1)}, bf16[512,512]{1,0:T(8,128)(2,1)}, u32[]{:S(2)}) copy-start(bf16[512,512]{1,0:T(8,128)(2,1)} %get-tuple-element.17) | copy-start | bytes 1572868
Sparse Core Ops, SparseCore 0:
  10.5 168.9 all-gather.3
  202.3 206.0 reduce-scatter.1
Sparse Core Ops, SparseCore 1:
  11.7 70.8 all-reduce.2
where the time goes:
time: 416 us
  blocking collectives  241 us (58%)
  waiting for transfers between devices  99.4 us (24%)
  matrix products  30.1 us (7%)
  other arithmetic  23.1 us (6%)
  between operations  16.3 us (4%)
  local copies, waits for them, and re-layouts  5.51 us (1%)
    unnamed x1, blocking collectives  158 us
    all_gather x1, blocking collectives, local(): lax.all_gather(gain_shard, 'fsdp', axis=0, tiled=True)  82.9 us
    all_gather x1, waiting for transfers between devices, local(): lax.all_gather(weight_shard, 'fsdp', axis=0, tiled=True)  80.9 us
    reduce_scatter x1, waiting for transfers between devices, local(): lax.psum_scatter(weight_term, 'fsdp', scatter_dimension=0, tiled=True)  17.3 us
    dot_general x1, matrix products, backward_piece(): lax.dot_general(kv_grad, weight_piece, (((1,), (1,)), ((), ())), preferre...  13.6 us
  transfers between devices with their start and end apart: 3, of which 2 were waited for; matrix products, arithmetic and copies ran while one was open for 14% of the time, Pallas kernels for 0%

commit v1 on v0

--- a/solution.py
+++ b/solution.py
@@ -3,6 +3,7 @@
 import jax.numpy as jnp
 from jax import lax
 from jax.sharding import PartitionSpec as P
+from jax.lax import all_to_all, axis_size
 
 HEAD = 128
 SEQ_LEN = 4096
@@ -11,6 +12,17 @@
 momentum_rate = 0.9
 outer_rate = 0.7
 mixing_rate = 0.5
+
+
+def produce_region_by_axis(dimension_no, x_part):
+    log = []
+    for _ in range(axis_size("fsdp")):
+        log.append(x_part)
+    v_now = jnp.stack(log, axis=0)
+    odd = jnp.concatenate(
+        all_to_all(v_now, axis_name="fsdp", split_axis=0, concat_axis=0), axis=dimension_no
+    )
+    return odd
 
 
 def angles_for(positions, head):
@@ -75,7 +87,7 @@
     kv_grad = jnp.concatenate([key_back, cotangent[:, kvw:]], axis=1)
     key_pre, hidden, gain_full = forward_piece(
         normed,
-        lax.all_gather(weight_shard, "fsdp", axis=0, tiled=True),
+        produce_region_by_axis(0, weight_shard),
         lax.all_gather(gain_shard, "fsdp", axis=0, tiled=True),
     )
     hidden_grad = backward_piece(kv_grad, lax.all_gather(weight_shard, "fsdp", axis=0, tiled=True))

time: 416 us -> 496 us (1.19)
  blocking collectives: 241 us -> 384 us
  waiting for transfers between devices: 99.4 us -> 22.7 us
  starting transfers between devices: 0.12 us -> 9.67 us
  local copies, waits for them, and re-layouts: 5.51 us -> 10.8 us
    all_gather x1, blocking collectives: 82.9 us -> 231 us  [local(): lax.all_gather(gain_shard, 'fsdp', axis=0, tiled=True)]
    all_gather x1, waiting for transfers between devices: 80.9 us -> 0.01 us  [local(): lax.all_gather(weight_shard, 'fsdp', axis=0, tiled=True)]
    all_to_all x0 -> x1, starting transfers between devices: none -> 9.55 us  [produce_region_by_axis(): all_to_all(v_now, axis_name='fsdp', split_axis=0, concat_axis=0)]
    another operation x0 -> x1, local copies, waits for them, and re-layouts: none -> 5.26 us  [produce_region_by_axis(): v_now = jnp.stack(log, axis=0)]
    unnamed x1, blocking collectives: 158 us -> 153 us
  transfers between devices with their start and end apart: 3 -> 4, of which waited for: 2 -> 1; matrix products, arithmetic and copies ran while one was open for 14% -> 12% of each run, Pallas kernels for 0% -> 0%
where the time goes in v1:
time: 496 us; the launch traced here: 495 us
  blocking collectives  384 us (77%)
  matrix products  28.3 us (6%)
  other arithmetic  23.1 us (5%)
  waiting for transfers between devices  22.7 us (5%)
  between operations  16.3 us (3%)
  local copies, waits for them, and re-layouts  10.8 us (2%)
  starting transfers between devices  9.67 us (2%)
    all_gather x1, blocking collectives, local(): lax.all_gather(gain_shard, 'fsdp', axis=0, tiled=True)  231 us
    unnamed x1, blocking collectives  153 us
    reduce_scatter x1, waiting for transfers between devices, local(): lax.psum_scatter(weight_term, 'fsdp', scatter_dimension=0, tiled=True)  21.4 us
    dot_general x1, matrix products, backward_piece(): lax.dot_general(kv_grad, weight_piece, (((1,), (1,)), ((), ())), preferre...  11.8 us
  transfers between devices with their start and end apart: 4, of which 1 were waited for; matrix products, arithmetic and copies ran while one was open for 12% of the time, Pallas kernels for 0%

profile of v1, /device:TPU:0, one launch (start us, length us, event | category | flops | bytes accessed | tf_op | source)
XLA Modules:
  0.0 495.3 jit_solution(16366300717158978435)
XLA Ops:
  8.0 0.7 all-reduce.3.cloned.1.call-update
  8.8 0.5 all-gather.4.cloned.1.call-update
  9.3 5.3 %stack.3 = bf16[32,128,1024]{2,1,0:T(8,128)(2,1)} broadcast(bf16[128,1024]{1,0:T(8,128)(2,1)} %bitcast.64), dimensions={1,2} | broadcast | bytes 8650752 | tf_op jit(solution)/shard_map/stack | solution.py:21
  14.6 9.5 %all-to-all-start = ((bf16[32,128,1024]{2,1,0:T(8,128)(2,1)}), bf16[32,128,1024]{2,1,0:T(8,128)(2,1)}, u32[]{:S(2)}, u32[]{:S(2)}) async-start(bf16[32,128,1024]{2,1,0:T(8,128)(2,1)} %stack.3), calls=%async_computation | async-start | bytes 16777216 | tf_op jit(solution)/shard_map/all_to_all | solution.py:23
  24.2 231.1 %all-gather = bf16[1,4096]{1,0:T(2,128)(2,1)S(1)} all-gather(bf16[1,128]{1,0:T(2,128)(2,1)S(1)} %copy-done.7), channel_id=2, replica_groups=mesh['replica'=4,'fsdp'=32] {'fsdp'}, dimensions={1}, use_global_device_ids=true | all-gather | bytes 8448 | tf_op jit(solution)/shard_map/all_gather | solution.py:91
  255.4 0.9 slice_convert_fusion.1
  256.7 3.1 fusion.12
  259.8 2.0 broadcast_multiply_fusion.1
  261.8 8.2 %fusion.18 = f32[512,1024]{1,0:T(8,128)S(1)} fusion(bf16[4096,1024]{1,0:T(8,128)(2,1)} %bitcast.4, bf16[1,512,4096]{2,1,0:T(8,128)(2,1)} %param.8, f32[4096]{0:T(1024)S(1)} %bitcast.68, f32[512]{0:T(512)S(1)} %add_rsqrt_fusion), kind=kOutput, calls=%fused_computation.21 | convolution fusion | flops 4303355904 | bytes 14698496 | tf_op jit(solution)/shard_map/dot_general | solution.py:51
  270.0 1.3 copy-done.2
  271.4 0.4 reshape.186
  271.8 2.7 subtract_convert_fusion
  274.6 1.4 pad_maximum_fusion.4
  276.1 8.3 %broadcast_multiply_fusion = f32[4096,1024]{1,0:T(8,128)} fusion(bf16[1,512,4096]{2,1,0:T(8,128)(2,1)S(1)} %copy-done, f32[4096]{0:T(1024)S(1)} %bitcast.69, f32[512]{0:T(512)S(1)} %add_rsqrt_fusion, bf16[512,512]{1,0:T(8,128)(2,1)S(1)} %copy-done.5, bf16[512,512]{1,0:T(8,128)(2,1)S(1)} %bitcast.66), kind=kOutput, calls=%fused_computation.19 | convolution fusion | flops 4309647360 | bytes 22038528 | tf_op jit(solution)/shard_map/dot_general | solution.py:100
  284.4 0.6 copy-done.8
  285.1 0.6 dynamic-slice
  286.3 4.6 fusion.28
  291.1 1.3 fusion.29
  292.4 1.1 pad_maximum_fusion
  293.5 11.8 %fusion.11 = (f32[4096]{0:T(1024)S(1)}, f32[512]{0:T(512)S(1)}, f32[512,4096]{1,0:T(8,128)}) fusion(bf16[1,512,4096]{2,1,0:T(8,128)(2,1)} %param.8, f32[512]{0:T(512)S(1)} %add_rsqrt_fusion, f32[4096]{0:T(1024)S(1)} %bitcast.70, bf16[1,4096,1024]{2,1,0:T(8,128)(2,1)} %all-gather.4.cloned.1.call-done, bf16[512,512]{1,0:T(8,128)(2,1)S(1)} %copy-done.6, ...), kind=kOutput, calls=%fused_computation.13 | convolution fusion | flops 4311739904 | bytes 22056960 | tf_op jit(solution)/shard_map/dot_general | solution.py:56
  305.3 153.3 %all-reduce = f32[4096]{0:T(1024)S(1)} all-reduce(f32[4096]{0:T(1024)S(1)} %broadcast_multiply_fusion.2), channel_id=5, replica_groups=mesh['replica'=4,'fsdp'=32] {'fsdp'}, use_global_device_ids=true, to_apply=%region_4.5.clone | all-reduce | flops 4096 | bytes 32768
  458.6 0.6 dynamic-slice_bitcast_fusion
  459.2 7.3 %fusion.21 = bf16[1,512,4096]{2,1,0:T(8,128)(2,1)} fusion(bf16[1,512,4096]{2,1,0:T(8,128)(2,1)} %param.8, f32[512,4096]{1,0:T(8,128)} %get-tuple-element.23, f32[512]{0:T(512)S(1)} %broadcast_multiply_fusion.3, f32[4096]{0:T(1024)S(1)} %bitcast.71, f32[512]{0:T(512)S(1)} %add_rsqrt_fusion), kind=kLoop, calls=%fused_computation.22 | loop fusion | flops 14680064 | bytes 16797696 | tf_op jit(solution)/shard_map/broadcast_in_dim | solution.py:125
  466.5 21.4 %reduce-scatter.2.cloned.1.call-done = f32[128,1024]{1,0:T(8,128)} async-done(((f32[4096,1024]{1,0:T(8,128)}), f32[128,1024]{1,0:T(8,128)}) %reduce-scatter.2.cloned.1.call-update) | async-done | bytes 524304 | tf_op jit(solution)/shard_map/reduce_scatter | solution.py:107
  (33 shorter events, 1.0 us)
Async XLA Ops:
  8.0 278.3 %all-reduce.3.cloned.1.call-start = ((), (), s32[]{:S(2)}) async-start(), calls=%async_computation.3 | async-start | bytes 3145728 | tf_op jit(solution)/shard_map/psum | solution.py:116
  8.7 284.8 %all-gather.4.cloned.1.call-start = ((), (), s32[]{:S(2)}) async-start(), calls=%async_computation.4 | async-start | bytes 8650752 | tf_op jit(solution)/shard_map/all_gather | solution.py:93
  14.6 9.6 %copy-start.7 = (bf16[1,128]{1,0:T(2,128)(2,1)S(1)}, bf16[1,128]{1,0:T(2,128)(2,1)}, u32[]{:S(2)}) copy-start(bf16[1,128]{1,0:T(2,128)(2,1)} %param.9) | copy-start | bytes 772
  14.6 240.8 %copy-start.3 = (bf16[1,512,1024]{2,1,0:T(8,128)(2,1)S(1)}, bf16[1,512,1024]{2,1,0:T(8,128)(2,1)}, u32[]{:S(2)}) copy-start(bf16[1,512,1024]{2,1,0:T(8,128)(2,1)} %param.11) | copy-start | bytes 3145732
  14.6 247.2 %all-to-all-start = ((bf16[32,128,1024]{2,1,0:T(8,128)(2,1)}), bf16[32,128,1024]{2,1,0:T(8,128)(2,1)}, u32[]{:S(2)}, u32[]{:S(2)}) async-start(bf16[32,128,1024]{2,1,0:T(8,128)(2,1)} %stack.3), calls=%async_computation | async-start | bytes 16777216 | tf_op jit(solution)/shard_map/all_to_all | solution.py:23
  24.1 463.8 %reduce-scatter.2.cloned.1.call-start = ((), (), s32[]{:S(2)}) async-start(), calls=%async_computation.2 | async-start | bytes 17301504 | tf_op jit(solution)/shard_map/reduce_scatter | solution.py:107
  270.0 1.3 copy-start.2
  271.8 4.3 copy-start
  271.8 4.3 copy-start.5
  284.4 0.7 copy-start.8
  284.4 1.9 copy-start.1
  284.4 1.9 copy-start.4
  290.9 2.6 copy-start.6
Sparse Core Ops, SparseCore 0:
  11.3 175.1 all-reduce.2
Sparse Core Ops, SparseCore 1:
  10.9 244.1 all-gather.3
  284.5 203.3 reduce-scatter.1
